TPU v7x, 32 devices: a whole 2x2x4 slice. The times are simulated.
32 devices in a mesh: ctx: 8 (over y, x, core), tp: 4 (over z).
Axes of the slice: x: 2, y: 2, z: 4, core: 2. Of those that a mesh axis runs over, the one named last changes fastest.
Arguments:
- query_mr: bfloat16 [2048, 8192], P('ctx', 'tp'), may hold values from -6 to 6
- key_mr: bfloat16 [2048, 8192], P('ctx', 'tp'), may hold values from -6 to 6
- value_mr: bfloat16 [2048, 8192], P('ctx', 'tp'), may hold values from -6 to 6
- query_li: bfloat16 [2048, 8192], P('ctx', 'tp'), may hold values from -6 to 6
- key_li: bfloat16 [2048, 8192], P('ctx', 'tp'), may hold values from -6 to 6
- cotangent: bfloat16 [2048, 8192], P('ctx', 'tp'), may hold values from -6 to 6
- mr_taps: float32 [128, 8192], P(None, 'tp'), may hold values from -0.5 to 0.5
- decay_rates: float32 [8], replicated, may hold values from 4.8828126e-05 to 0.03
- residues: float32 [8, 8192], P(None, 'tp'), may hold values from -2 to 2
Outputs:
- grad_query_mr: bfloat16 [2048, 8192], P('ctx', 'tp')
- grad_key_mr: bfloat16 [2048, 8192], P('ctx', 'tp')
- grad_value_mr: bfloat16 [2048, 8192], P('ctx', 'tp')
- grad_query_li: bfloat16 [2048, 8192], P('ctx', 'tp')
- grad_key_li: bfloat16 [2048, 8192], P('ctx', 'tp')
- grad_taps: float32 [128, 8192], P(None, 'tp')
- grad_residues: float32 [8, 8192], P(None, 'tp')
All inputs are finite; a program needn't handle non-finite values.
Results may differ from a plain program's by a relative error of at most 0.001.
Values may be sent and summed in bfloat16 or wider, within the bound.
A program may use at most 128 MiB of HBM per device.

v0:
```python
import math
import jax
import jax.numpy as jnp
from jax import lax
from jax.sharding import PartitionSpec as P

BLOCK = 128
highest = lax.Precision.HIGHEST


def from_behind(value, axis, by):
    size = lax.axis_size(axis)
    pairs = [(i, i + by) for i in range(size) if 0 <= i + by < size]
    return lax.ppermute(value, axis, pairs)


def depthwise(signal, kernel):
    channels = signal.shape[1]
    output = lax.conv_general_dilated(
        signal[None],
        kernel[:, None, :],
        (1,),
        "VALID",
        dimension_numbers=("NWC", "WIO", "NWC"),
        feature_group_count=channels,
        precision=highest,
    )
    return output[0]


def linked(earlier, later):
    return (earlier[0] * later[1] + later[0], earlier[1] * later[1])


def modal_terms(inputs, cotangents, decay_rates, residues, block_len):
    length, channels = inputs.shape
    blocks = length // block_len
    in_blocks = inputs.reshape(blocks, block_len, channels)
    co_blocks = cotangents.reshape(blocks, block_len, channels)
    places = jnp.arange(block_len, dtype=jnp.float32)
    offsets = places[:, None] - places[None, :]
    modes = decay_rates.shape[0]

    def one_mode(mode, state):
        conv_sum, back_sum, residue_grad, end_rows, start_rows = state
        decay_rate = decay_rates[mode]
        residue_row = lax.dynamic_index_in_dim(residues, mode, 0, keepdims=False)
        mode_scale = jnp.sqrt(-jnp.expm1(-2.0 * decay_rate))
        toeplitz = jnp.where(
            offsets >= 0.0, mode_scale * jnp.exp(-decay_rate * jnp.maximum(offsets, 0.0)), 0.0
        )
        block_pows = jnp.full((blocks, 1), jnp.exp(-decay_rate * block_len), jnp.float32)
        forward = jnp.einsum("tj,bjc->btc", toeplitz, in_blocks, precision=highest)
        backward = jnp.einsum("jt,bjc->btc", toeplitz, co_blocks, precision=highest)
        forward_incl = lax.associative_scan(linked, (forward[:, -1], block_pows))[0]
        backward_incl = lax.associative_scan(linked, (backward[:, 0], block_pows), reverse=True)[0]
        zero_row = jnp.zeros((1, channels), jnp.float32)
        forward_in = jnp.concatenate([zero_row, forward_incl[:-1]], 0)
        backward_in = jnp.concatenate([backward_incl[1:], zero_row], 0)
        lead_pows = jnp.exp(-decay_rate * (places + 1.0))
        tail_pows = jnp.exp(-decay_rate * (block_len - places))
        states = (forward + lead_pows[None, :, None] * forward_in[:, None, :]).reshape(
            length, channels
        )
        reverse_states = (backward + tail_pows[None, :, None] * backward_in[:, None, :]).reshape(
            length, channels
        )
        conv_sum = conv_sum + residue_row[None, :] * states
        back_sum = back_sum + residue_row[None, :] * reverse_states
        residue_grad = lax.dynamic_update_index_in_dim(
            residue_grad, jnp.sum(inputs * reverse_states, 0), mode, 0
        )
        end_rows = lax.dynamic_update_index_in_dim(end_rows, states[length - 1], mode, 0)
        start_rows = lax.dynamic_update_index_in_dim(start_rows, reverse_states[0], mode, 0)
        return (conv_sum, back_sum, residue_grad, end_rows, start_rows)

    zero_field = jnp.zeros((length, channels), jnp.float32)
    zero_modes = jnp.zeros((modes, channels), jnp.float32)
    return lax.fori_loop(
        0, modes, one_mode, (zero_field, zero_field, zero_modes, zero_modes, zero_modes)
    )


def per_device(
    query_mr, key_mr, value_mr, query_li, key_li, cotangent, mr_taps, decay_rates, residues
):
    length, channels = query_mr.shape
    taps_len = mr_taps.shape[0]
    rim_rows = taps_len - 1
    devices_ctx = lax.axis_size("ctx")
    seq_len = length * devices_ctx
    prior_key, prior_value = from_behind(
        (key_mr[length - rim_rows :], value_mr[length - rim_rows :]), "ctx", 1
    )
    key_first = key_mr.astype(jnp.float32)
    value_first = value_mr.astype(jnp.float32)
    query_first = query_mr.astype(jnp.float32)
    mixed_in = jnp.concatenate([prior_key, key_mr], 0).astype(jnp.float32) * jnp.concatenate(
        [prior_value, value_mr], 0
    ).astype(jnp.float32)
    mr_conv = depthwise(mixed_in, mr_taps[::-1])
    mr_out = query_first * mr_conv
    key_second = key_li.astype(jnp.float32)
    cotan = cotangent.astype(jnp.float32)
    li_input = key_second * mr_out
    li_cotan = cotan * query_li.astype(jnp.float32)
    regrouped = lax.all_to_all(
        jnp.stack([li_input, li_cotan]), "ctx", split_axis=2, concat_axis=1, tiled=True
    )
    piece_cols = channels // devices_ctx
    local_residues = lax.dynamic_slice_in_dim(
        residues, lax.axis_index("ctx") * piece_cols, piece_cols, 1
    )
    conv_seq, back_seq, residue_piece, unused_ends, unused_starts = modal_terms(
        regrouped[0], regrouped[1], decay_rates, local_residues, BLOCK
    )
    returned = lax.all_to_all(
        jnp.stack([conv_seq, back_seq]), "ctx", split_axis=1, concat_axis=2, tiled=True
    )
    li_conv = returned[0]
    li_back = returned[1]
    residue_sum = lax.all_gather(residue_piece, "ctx", axis=1, tiled=True)
    grad_query_li = (cotan * li_conv).astype(jnp.bfloat16)
    grad_key_li = (mr_out * li_back).astype(jnp.bfloat16)
    mr_grad = cotan + key_second * li_back
    grad_query_mr = (mr_grad * mr_conv).astype(jnp.bfloat16)
    mr_cotan = mr_grad * query_first
    next_rows = from_behind(mr_cotan[:rim_rows], "ctx", -1)
    mixed_grad = depthwise(jnp.concatenate([mr_cotan, next_rows], 0), mr_taps)
    grad_key_mr = (mixed_grad * value_first).astype(jnp.bfloat16)
    grad_value_mr = (mixed_grad * key_first).astype(jnp.bfloat16)
    tap_part = depthwise(mixed_in, mr_cotan)[::-1]
    tap_sum = lax.psum(tap_part, "ctx")
    factor = 1.0 / math.sqrt(seq_len)
    return (
        grad_query_mr,
        grad_key_mr,
        grad_value_mr,
        grad_query_li,
        grad_key_li,
        tap_sum * factor,
        residue_sum * factor,
    )


def solution(mesh):
    placed = (
        P("ctx", "tp"),
        P("ctx", "tp"),
        P("ctx", "tp"),
        P("ctx", "tp"),
        P("ctx", "tp"),
        P("ctx", "tp"),
        P(None, "tp"),
        P(),
        P(None, "tp"),
    )
    return jax.shard_map(
        per_device,
        mesh=mesh,
        in_specs=placed,
        out_specs=(
            P("ctx", "tp"),
            P("ctx", "tp"),
            P("ctx", "tp"),
            P("ctx", "tp"),
            P("ctx", "tp"),
            P(None, "tp"),
            P(None, "tp"),
        ),
        check_vma=False,
    )
```

profile of v0, /device:TPU:0, one launch (start us, length us, event | category | flops | bytes accessed | tf_op | source)
XLA Modules:
  0.0 570.9 jit_solution(17721856543120809470)
XLA Ops:
  9.3 2.4 collective-permute-start
  13.7 5.3 collective-permute-start.1
  19.0 8.9 %rev.15 = f32[128,2048]{1,0:T(8,128)} reverse(f32[128,2048]{1,0:T(8,128)} %param.17), dimensions={0} | reverse | bytes 2097152 | tf_op jit(solution)/shard_map/rev | solution.py:101
  31.3 21.5 %fusion.49 = f32[1,256,2048]{2,0,1:T(1,128)S(1)} fusion(f32[1,383,2048]{2,1,0:T(8,128)S(1)} %convert_multiply_fusion, f32[128,1,2048]{2,0,1:T(8,128)S(1)} %bitcast.140), kind=kOutput, calls=%fused_computation.100 | convolution fusion | flops 805306368 | bytes 6283264 | tf_op jit(solution)/shard_map/conv_general_dilated | solution.py:19
  54.4 2.5 pad_maximum_fusion.6
  56.9 7.3 %copy.48 = f32[2,256,2048]{1,0,2:T(2,128)} copy(f32[2,256,2048]{2,1,0:T(8,128)} %pad_maximum_fusion.6) | data formatting | bytes 8388608 | tf_op jit(solution)/shard_map/stack | solution.py:108
  64.1 4.6 all-to-all-start
  68.8 49.0 %all-to-all-done = f32[2,256,2048]{1,0,2:T(2,128)} async-done(((f32[2,256,2048]{1,0,2:T(2,128)}), f32[2,256,2048]{1,0,2:T(2,128)}, u32[]{:S(2)}, u32[]{:S(2)}) %all-to-all-start) | async-done | bytes 4194336 | tf_op jit(solution)/shard_map/all_to_all | solution.py:107
  117.8 9.6 %fusion.58 = (f32[1,8,256,256]{2,0,3,1:T(1,128)}, f32[1,8,256,256]{2,0,3,1:T(1,128)}) fusion(f32[2,8,256,256]{2,0,3,1:T(2,128)} %bitcast.8), kind=kLoop, calls=%fused_computation.113 | loop fusion | bytes 8388608 | tf_op jit(solution)/shard_map/slice | solution.py:115
  127.4 4.5 copy.49
  131.9 6.0 %copy.50 = f32[1,8,256,256]{3,2,1,0:T(8,128)} copy(f32[1,8,256,256]{2,0,3,1:T(1,128)} %get-tuple-element.304) | data formatting | bytes 4194304 | tf_op jit(solution)/shard_map/slice | solution.py:115
  138.0 240.8 %while.19 = (s32[]{:T(128)}, f32[2048,256]{1,0:T(8,128)}, f32[2048,256]{1,0:T(8,128)}, f32[8,256]{1,0:T(8,128)S(1)}, f32[8,256]{1,0:T(8,128)S(1)}, /*index=5*/f3...) while((s32[]{:T(128)}, f32[2048,256]{1,0:T(8,128)}, ...), condition=%wide.region_2.3_spmd.clone.clone, body=%wide.region_0.2_spmd.clone.clone.sunk | while | flops 1617155328 | bytes 74435056 | solution.py:79
  143.8 3.5 fusion.80
  151.2 3.3 multiply_add_fusion.22
  155.4 4.0 fusion.89
  159.4 2.6 copy.106
  162.0 4.9 fusion.90
  172.8 3.5 fusion.80
  180.3 3.3 multiply_add_fusion.22
  184.4 4.0 fusion.89
  188.4 2.6 copy.106
  191.0 6.2 %fusion.90 = (f32[2048,256]{1,0:T(8,128)}, f32[2048,256]{1,0:T(8,128)}) fusion(f32[16,128,256]{2,1,0:T(8,128)} %copy.106, f32[2048,256]{1,0:T(8,128)} %get-tuple-element.414, f32[256]{0:T(256)S(1)} %bitcast.142, pred[]{:T(512)S(6)} %compare.24, f32[16,128,256]{2,1,0:T(8,128)} %multiply_add_fusion.22, f32[2048,256]{1,0:T(8,128)} %get-tuple-element.413), kind=kLoop, calls=%fused_computation.3.clone.1 | loop fusion | flops 3145728 | bytes 12583937 | tf_op jit(solution)/shard_map/while/body/eval_jaxpr/add | solution.py:69
  203.0 3.5 fusion.80
  210.5 3.3 multiply_add_fusion.22
  214.6 4.0 fusion.89
  218.7 2.6 copy.106
  221.3 6.2 %fusion.90 = (f32[2048,256]{1,0:T(8,128)}, f32[2048,256]{1,0:T(8,128)}) fusion(f32[16,128,256]{2,1,0:T(8,128)} %copy.106, f32[2048,256]{1,0:T(8,128)} %get-tuple-element.414, f32[256]{0:T(256)S(1)} %bitcast.142, pred[]{:T(512)S(6)} %compare.24, f32[16,128,256]{2,1,0:T(8,128)} %multiply_add_fusion.22, f32[2048,256]{1,0:T(8,128)} %get-tuple-element.413), kind=kLoop, calls=%fused_computation.3.clone.1 | loop fusion | flops 3145728 | bytes 12583937 | tf_op jit(solution)/shard_map/while/body/eval_jaxpr/add | solution.py:69
  233.3 3.5 fusion.80
  240.8 3.3 multiply_add_fusion.22
  244.9 4.0 fusion.89
  248.9 2.6 copy.106
  251.5 6.2 %fusion.90 = (f32[2048,256]{1,0:T(8,128)}, f32[2048,256]{1,0:T(8,128)}) fusion(f32[16,128,256]{2,1,0:T(8,128)} %copy.106, f32[2048,256]{1,0:T(8,128)} %get-tuple-element.414, f32[256]{0:T(256)S(1)} %bitcast.142, pred[]{:T(512)S(6)} %compare.24, f32[16,128,256]{2,1,0:T(8,128)} %multiply_add_fusion.22, f32[2048,256]{1,0:T(8,128)} %get-tuple-element.413), kind=kLoop, calls=%fused_computation.3.clone.1 | loop fusion | flops 3145728 | bytes 12583937 | tf_op jit(solution)/shard_map/while/body/eval_jaxpr/add | solution.py:69
  263.6 3.5 fusion.80
  271.0 3.3 multiply_add_fusion.22
  275.2 4.0 fusion.89
  279.2 2.6 copy.106
  281.8 6.2 %fusion.90 = (f32[2048,256]{1,0:T(8,128)}, f32[2048,256]{1,0:T(8,128)}) fusion(f32[16,128,256]{2,1,0:T(8,128)} %copy.106, f32[2048,256]{1,0:T(8,128)} %get-tuple-element.414, f32[256]{0:T(256)S(1)} %bitcast.142, pred[]{:T(512)S(6)} %compare.24, f32[16,128,256]{2,1,0:T(8,128)} %multiply_add_fusion.22, f32[2048,256]{1,0:T(8,128)} %get-tuple-element.413), kind=kLoop, calls=%fused_computation.3.clone.1 | loop fusion | flops 3145728 | bytes 12583937 | tf_op jit(solution)/shard_map/while/body/eval_jaxpr/add | solution.py:69
  293.8 3.5 fusion.80
  301.3 3.3 multiply_add_fusion.22
  305.4 4.0 fusion.89
  309.4 2.6 copy.106
  312.0 6.2 %fusion.90 = (f32[2048,256]{1,0:T(8,128)}, f32[2048,256]{1,0:T(8,128)}) fusion(f32[16,128,256]{2,1,0:T(8,128)} %copy.106, f32[2048,256]{1,0:T(8,128)} %get-tuple-element.414, f32[256]{0:T(256)S(1)} %bitcast.142, pred[]{:T(512)S(6)} %compare.24, f32[16,128,256]{2,1,0:T(8,128)} %multiply_add_fusion.22, f32[2048,256]{1,0:T(8,128)} %get-tuple-element.413), kind=kLoop, calls=%fused_computation.3.clone.1 | loop fusion | flops 3145728 | bytes 12583937 | tf_op jit(solution)/shard_map/while/body/eval_jaxpr/add | solution.py:69
  324.1 3.5 fusion.80
  331.5 3.3 multiply_add_fusion.22
  335.7 4.0 fusion.89
  339.7 2.6 copy.106
  342.3 6.2 %fusion.90 = (f32[2048,256]{1,0:T(8,128)}, f32[2048,256]{1,0:T(8,128)}) fusion(f32[16,128,256]{2,1,0:T(8,128)} %copy.106, f32[2048,256]{1,0:T(8,128)} %get-tuple-element.414, f32[256]{0:T(256)S(1)} %bitcast.142, pred[]{:T(512)S(6)} %compare.24, f32[16,128,256]{2,1,0:T(8,128)} %multiply_add_fusion.22, f32[2048,256]{1,0:T(8,128)} %get-tuple-element.413), kind=kLoop, calls=%fused_computation.3.clone.1 | loop fusion | flops 3145728 | bytes 12583937 | tf_op jit(solution)/shard_map/while/body/eval_jaxpr/add | solution.py:69
  354.3 3.5 fusion.80
  361.8 3.3 multiply_add_fusion.22
  365.9 4.0 fusion.89
  369.9 2.6 copy.106
  372.6 6.2 %fusion.90 = (f32[2048,256]{1,0:T(8,128)}, f32[2048,256]{1,0:T(8,128)}) fusion(f32[16,128,256]{2,1,0:T(8,128)} %copy.106, f32[2048,256]{1,0:T(8,128)} %get-tuple-element.414, f32[256]{0:T(256)S(1)} %bitcast.142, pred[]{:T(512)S(6)} %compare.24, f32[16,128,256]{2,1,0:T(8,128)} %multiply_add_fusion.22, f32[2048,256]{1,0:T(8,128)} %get-tuple-element.413), kind=kLoop, calls=%fused_computation.3.clone.1 | loop fusion | flops 3145728 | bytes 12583937 | tf_op jit(solution)/shard_map/while/body/eval_jaxpr/add | solution.py:69
  378.8 3.4 stack.21
  383.7 4.1 pad_maximum_fusion.7
  387.8 51.5 %all_to_all.30 = f32[2,2048,256]{2,0,1:T(2,128)S(1)} all-to-all(f32[2,2048,256]{2,0,1:T(2,128)S(1)} %pad_maximum_fusion.7), channel_id=1, replica_groups=mesh['ctx'=8,'tp'=4] {'ctx'}, dimensions={1} | all-to-all | bytes 8388608 | tf_op jit(solution)/shard_map/all_to_all | solution.py:117
  439.3 2.4 copy.97
  445.1 3.5 multiply_convert_fusion
  450.9 21.4 %fusion.46 = f32[1,128,2048]{2,0,1:T(1,128)S(1)} fusion(f32[256,1,2048]{2,0,1:T(8,128)S(1)} %bitcast.128, f32[1,383,2048]{2,1,0:T(8,128)S(1)} %copy-done.19), kind=kOutput, calls=%fused_computation.96 | convolution fusion | flops 805306368 | bytes 6283264 | tf_op jit(solution)/shard_map/conv_general_dilated | solution.py:19
  472.7 5.2 rev.16
  477.9 9.9 %all_gather.3 = f32[8,2048]{1,0:T(8,128)S(1)} all-gather(f32[8,256]{1,0:T(8,128)S(1)} %get-tuple-element.201), channel_id=1, replica_groups=mesh['ctx'=8,'tp'=4] {'ctx'}, dimensions={1}, use_global_device_ids=true | all-gather | bytes 73728 | tf_op jit(solution)/shard_map/all_gather | solution.py:122
  488.4 47.4 %all-reduce.20.cloned.1.call-done = f32[128,2048]{1,0:T(8,128)} async-done(((f32[128,2048]{1,0:T(8,128)}), f32[128,2048]{1,0:T(8,128)}) %all-reduce.20.cloned.1.call-update) | async-done | bytes 1048592 | tf_op jit(solution)/shard_map/psum | solution.py:133
  535.8 2.3 broadcast_multiply_fusion
  539.7 21.8 %fusion.38 = f32[1,256,2048]{2,0,1:T(1,128)S(1)} fusion(f32[1,383,2048]{2,1,0:T(8,128)S(1)} %maximum_bitcast_fusion, f32[128,1,2048]{2,0,1:T(8,128)S(1)} %bitcast.139), kind=kOutput, calls=%fused_computation.81 | convolution fusion | flops 805306368 | bytes 6283264 | tf_op jit(solution)/shard_map/conv_general_dilated | solution.py:19
  561.5 2.5 fusion.44
  (718 shorter events, 90.4 us)
Async XLA Ops:
  7.2 61.6 %copy-start = (f32[8,2048]{1,0:T(8,128)S(1)}, f32[8,2048]{1,0:T(8,128)}, u32[]{:S(2)}) copy-start(f32[8,2048]{1,0:T(8,128)} %param.19) | copy-start | bytes 196612
  7.2 20.7 %copy-start.9 = (bf16[256,2048]{1,0:T(8,128)(2,1)S(1)}, bf16[256,2048]{1,0:T(8,128)(2,1)}, u32[]{:S(2)}) copy-start(bf16[256,2048]{1,0:T(8,128)(2,1)} %param.12) | copy-start | bytes 3145732
  7.2 20.7 %copy-start.11 = (bf16[256,2048]{1,0:T(8,128)(2,1)S(1)}, bf16[256,2048]{1,0:T(8,128)(2,1)}, u32[]{:S(2)}) copy-start(bf16[256,2048]{1,0:T(8,128)(2,1)} %param.13) | copy-start | bytes 3145732
  9.3 18.5 %collective-permute-start = (bf16[127,2048]{1,0:T(8,128)(2,1)}, bf16[127,2048]{1,0:T(8,128)(2,1)S(1)}, u32[]{:S(2)}, u32[]{:S(2)}) collective-permute-start(bf16[127,2048]{1,0:T(8,128)(2,1)} %slice.393), channel_id=1, source_target_pairs={{0,4},{4,8},{8,12},{12,16},{16,20},{20,24},{24,28},{1,5},{5,9},{9,... | collective-permute-start | bytes 1560584 | tf_op jit(solution)/shard_map/ppermute | solution.py:14
  13.7 14.1 %collective-permute-start.1 = (bf16[127,2048]{1,0:T(8,128)(2,1)}, bf16[127,2048]{1,0:T(8,128)(2,1)}, u32[]{:S(2)}, u32[]{:S(2)}) collective-permute-start(bf16[127,2048]{1,0:T(8,128)(2,1)} %slice.394), channel_id=1, source_target_pairs={{0,4},{4,8},{8,12},{12,16},{16,20},{20,24},{24,28},{1,5},{5,9},{9,... | collective-permute-start | bytes 1560584 | tf_op jit(solution)/shard_map/ppermute | solution.py:14
  27.9 3.4 copy-start.22
  29.6 1.6 copy-start.18
  31.3 21.6 %copy-start.13 = (bf16[256,2048]{1,0:T(8,128)(2,1)S(1)}, bf16[256,2048]{1,0:T(8,128)(2,1)}, u32[]{:S(2)}) copy-start(bf16[256,2048]{1,0:T(8,128)(2,1)} %param.15) | copy-start | bytes 3145732
  31.3 21.6 %copy-start.14 = (bf16[256,2048]{1,0:T(8,128)(2,1)S(1)}, bf16[256,2048]{1,0:T(8,128)(2,1)}, u32[]{:S(2)}) copy-start(bf16[256,2048]{1,0:T(8,128)(2,1)} %param.11) | copy-start | bytes 3145732
  31.3 21.6 %copy-start.16 = (bf16[256,2048]{1,0:T(8,128)(2,1)S(1)}, bf16[256,2048]{1,0:T(8,128)(2,1)}, u32[]{:S(2)}) copy-start(bf16[256,2048]{1,0:T(8,128)(2,1)} %param.16) | copy-start | bytes 3145732
  31.3 21.6 %copy-start.20 = (bf16[256,2048]{1,0:T(8,128)(2,1)S(1)}, bf16[256,2048]{1,0:T(8,128)(2,1)}, u32[]{:S(2)}) copy-start(bf16[256,2048]{1,0:T(8,128)(2,1)} %param.14) | copy-start | bytes 3145732
  52.9 1.5 copy-start.7
  64.1 53.7 %all-to-all-start = ((f32[2,256,2048]{1,0,2:T(2,128)}), f32[2,256,2048]{1,0,2:T(2,128)}, u32[]{:S(2)}, u32[]{:S(2)}) async-start(f32[2,256,2048]{1,0,2:T(2,128)} %copy.48), calls=%async_computation | async-start | bytes 8388608 | tf_op jit(solution)/shard_map/all_to_all | solution.py:107
  68.7 467.2 %all-reduce.20.cloned.1.call-start = ((), (), s32[]{:S(2)}) async-start(), calls=%async_computation.2 | async-start | bytes 2097152 | tf_op jit(solution)/shard_map/psum | solution.py:133
  131.9 6.1 %copy-start.23 = (f32[8]{0:T(128)S(1)}, f32[8]{0:T(128)}, u32[]{:S(2)}) copy-start(f32[8]{0:T(128)} %param.18) | copy-start | bytes 100
  138.0 4.1 copy-start.2
  142.1 1.3 copy-start.4
  148.5 1.4 copy-start.6
  162.0 5.0 copy-start.3
  167.0 4.1 copy-start.2
  171.1 1.3 copy-start.4
  177.5 1.4 copy-start.6
  191.0 6.2 %copy-start.3 = (f32[2048,256]{1,0:T(8,128)S(1)}, f32[2048,256]{1,0:T(8,128)}, u32[]{:S(2)}) copy-start(f32[2048,256]{1,0:T(8,128)} %copy-done.2) | copy-start | bytes 6291460 | tf_op jit(solution)/shard_map/while
  197.2 4.1 copy-start.2
  201.3 1.3 copy-start.4
  207.8 1.4 copy-start.6
  221.3 6.2 %copy-start.3 = (f32[2048,256]{1,0:T(8,128)S(1)}, f32[2048,256]{1,0:T(8,128)}, u32[]{:S(2)}) copy-start(f32[2048,256]{1,0:T(8,128)} %copy-done.2) | copy-start | bytes 6291460 | tf_op jit(solution)/shard_map/while
  227.5 4.1 copy-start.2
  231.6 1.3 copy-start.4
  238.0 1.4 copy-start.6
  251.5 6.2 %copy-start.3 = (f32[2048,256]{1,0:T(8,128)S(1)}, f32[2048,256]{1,0:T(8,128)}, u32[]{:S(2)}) copy-start(f32[2048,256]{1,0:T(8,128)} %copy-done.2) | copy-start | bytes 6291460 | tf_op jit(solution)/shard_map/while
  257.8 4.1 copy-start.2
  261.8 1.3 copy-start.4
  268.3 1.4 copy-start.6
  281.8 6.2 %copy-start.3 = (f32[2048,256]{1,0:T(8,128)S(1)}, f32[2048,256]{1,0:T(8,128)}, u32[]{:S(2)}) copy-start(f32[2048,256]{1,0:T(8,128)} %copy-done.2) | copy-start | bytes 6291460 | tf_op jit(solution)/shard_map/while
  288.0 4.1 copy-start.2
  292.1 1.3 copy-start.4
  298.5 1.4 copy-start.6
  312.0 6.2 %copy-start.3 = (f32[2048,256]{1,0:T(8,128)S(1)}, f32[2048,256]{1,0:T(8,128)}, u32[]{:S(2)}) copy-start(f32[2048,256]{1,0:T(8,128)} %copy-done.2) | copy-start | bytes 6291460 | tf_op jit(solution)/shard_map/while
  318.3 4.1 copy-start.2
  322.4 1.3 copy-start.4
  328.8 1.4 copy-start.6
  342.3 6.2 %copy-start.3 = (f32[2048,256]{1,0:T(8,128)S(1)}, f32[2048,256]{1,0:T(8,128)}, u32[]{:S(2)}) copy-start(f32[2048,256]{1,0:T(8,128)} %copy-done.2) | copy-start | bytes 6291460 | tf_op jit(solution)/shard_map/while
  348.5 4.1 copy-start.2
  352.6 1.3 copy-start.4
  359.0 1.4 copy-start.6
  372.6 6.2 %copy-start.3 = (f32[2048,256]{1,0:T(8,128)S(1)}, f32[2048,256]{1,0:T(8,128)}, u32[]{:S(2)}) copy-start(f32[2048,256]{1,0:T(8,128)} %copy-done.2) | copy-start | bytes 6291460 | tf_op jit(solution)/shard_map/while
  378.8 3.4 copy-start.5
  442.9 1.6 copy-start.8
  442.9 1.8 copy-start.15
  443.0 2.1 copy-start.17
  445.1 5.8 %copy-start.19 = (f32[1,383,2048]{2,1,0:T(8,128)S(1)}, f32[1,383,2048]{2,1,0:T(8,128)}, u32[]{:S(2)}) copy-start(f32[1,383,2048]{2,1,0:T(8,128)} %copy-done.18) | copy-start | bytes 9412612
  449.6 88.5 %collective-permute-start.2 = (f32[127,2048]{1,0:T(8,128)}, f32[127,2048]{1,0:T(8,128)}, u32[]{:S(2)}, u32[]{:S(2)}) collective-permute-start(f32[127,2048]{1,0:T(8,128)} %slice.517), channel_id=1, source_target_pairs={{4,0},{8,4},{12,8},{16,12},{20,16},{24,20},{28,24},{5,1},{9,5},{13... | collective-permute-start | bytes 3121160 | tf_op jit(solution)/shard_map/ppermute | solution.py:14
  538.1 1.5 copy-start.21
  539.7 21.8 %copy-start.10 = (bf16[256,2048]{1,0:T(8,128)(2,1)S(1)}, bf16[256,2048]{1,0:T(8,128)(2,1)}, u32[]{:S(2)}) copy-start(bf16[256,2048]{1,0:T(8,128)(2,1)} %param.12) | copy-start | bytes 3145732
  539.7 21.8 %copy-start.12 = (bf16[256,2048]{1,0:T(8,128)(2,1)S(1)}, bf16[256,2048]{1,0:T(8,128)(2,1)}, u32[]{:S(2)}) copy-start(bf16[256,2048]{1,0:T(8,128)(2,1)} %param.13) | copy-start | bytes 3145732
  539.7 24.3 %copy-start.1 = (f32[8,2048]{1,0:T(8,128)S(1)}, f32[8,2048]{1,0:T(8,128)}, u32[]{:S(2)}) copy-start(f32[8,2048]{1,0:T(8,128)} %param.19) | copy-start | bytes 196612
Sparse Core Ops, SparseCore 0:
  478.0 57.7 all-reduce.19
where the time goes:
time: 574 us; the launch traced here: 571 us
  local copies, waits for them, and re-layouts  134 us (23%)
  other arithmetic  128 us (22%)
  matrix products  108 us (19%)
  waiting for transfers between devices  96.4 us (17%)
  blocking collectives  61.4 us (11%)
  between operations  14.4 us (3%)
  loops' own time  13.9 us (2%)
  starting transfers between devices  13.6 us (2%)
    conv_general_dilated x3, matrix products, depthwise(): lax.conv_general_dilated(signal[None], kernel[:, None, :], (1,), 'VALID',...  64.7 us
    all_to_all x1, blocking collectives, per_device(): lax.all_to_all(jnp.stack([conv_seq, back_seq]), 'ctx', split_axis=1, conc...  51.5 us
    all_to_all x1, waiting for transfers between devices, per_device(): lax.all_to_all(jnp.stack([li_input, li_cotan]), 'ctx', split_axis=2, conc...  49 us
    add x8, other arithmetic, one_mode(): back_sum = back_sum + residue_row[None, :] * reverse_states  48.2 us
    psum x1, waiting for transfers between devices, per_device(): tap_sum = lax.psum(tap_part, 'ctx')  47.4 us
    reduce_sum x8, other arithmetic, one_mode(): jnp.sum(inputs * reverse_states, 0)  32.1 us
    dot_general x8, matrix products, one_mode(): backward = jnp.einsum('jt,bjc->btc', toeplitz, co_blocks, precision=highest)  27.8 us
    add x8, other arithmetic, one_mode(): forward + lead_pows[None, :, None] * forward_in[:, None, :]  26.2 us
  transfers between devices with their start and end apart: 5, of which 2 were waited for; matrix products, arithmetic and copies ran while one was open for 7% of the time, Pallas kernels for 0%

commit v1 on v0

--- a/solution.py
+++ b/solution.py
@@ -130,7 +130,7 @@
     grad_key_mr = (mixed_grad * value_first).astype(jnp.bfloat16)
     grad_value_mr = (mixed_grad * key_first).astype(jnp.bfloat16)
     tap_part = depthwise(mixed_in, mr_cotan)[::-1]
-    tap_sum = lax.psum(tap_part, "ctx")
+    tap_sum = jax.lax.all_gather(tap_part, "ctx").sum(axis=0)
     factor = 1.0 / math.sqrt(seq_len)
     return (
         grad_query_mr,

time: 574 us -> 551 us (0.960)
  waiting for transfers between devices: 96.4 us -> 54.2 us
  blocking collectives: 61.4 us -> 79.5 us
    psum x1 -> x0, waiting for transfers between devices: 47.4 us -> none  [per_device(): tap_sum = lax.psum(tap_part, 'ctx')]
    all_gather x1, blocking collectives: 9.89 us -> 27.9 us  [per_device(): residue_sum = lax.all_gather(residue_piece, 'ctx', axis=1, tiled=True)]
where the time goes in v1:
time: 551 us; the launch traced here: 548 us
  local copies, waits for them, and re-layouts  134 us (24%)
  other arithmetic  130 us (24%)
  matrix products  108 us (20%)
  blocking collectives  79.5 us (14%)
  waiting for transfers between devices  54.2 us (10%)
  between operations  14.4 us (3%)
  loops' own time  13.9 us (3%)
  starting transfers between devices  13.6 us (2%)
    conv_general_dilated x3, matrix products, depthwise(): lax.conv_general_dilated(signal[None], kernel[:, None, :], (1,), 'VALID',...  64.3 us
    all_to_all x1, blocking collectives, per_device(): lax.all_to_all(jnp.stack([conv_seq, back_seq]), 'ctx', split_axis=1, conc...  51.5 us
    all_to_all x1, waiting for transfers between devices, per_device(): lax.all_to_all(jnp.stack([li_input, li_cotan]), 'ctx', split_axis=2, conc...  49 us
    add x8, other arithmetic, one_mode(): back_sum = back_sum + residue_row[None, :] * reverse_states  48.2 us
    reduce_sum x8, other arithmetic, one_mode(): jnp.sum(inputs * reverse_states, 0)  32.1 us
    all_gather x1, blocking collectives, per_device(): residue_sum = lax.all_gather(residue_piece, 'ctx', axis=1, tiled=True)  27.9 us
    dot_general x8, matrix products, one_mode(): backward = jnp.einsum('jt,bjc->btc', toeplitz, co_blocks, precision=highest)  27.8 us
    add x8, other arithmetic, one_mode(): forward + lead_pows[None, :, None] * forward_in[:, None, :]  26.2 us
  transfers between devices with their start and end apart: 5, of which 2 were waited for; matrix products, arithmetic and copies ran while one was open for 7% of the time, Pallas kernels for 0%

profile of v1, /device:TPU:0, one launch (start us, length us, event | category | flops | bytes accessed | tf_op | source)
XLA Modules:
  0.0 547.8 jit_solution(1416313584409371274)
XLA Ops:
  9.3 2.4 collective-permute-start
  13.7 5.3 collective-permute-start.1
  19.0 8.9 %rev.15 = f32[128,2048]{1,0:T(8,128)} reverse(f32[128,2048]{1,0:T(8,128)} %param.17), dimensions={0} | reverse | bytes 2097152 | tf_op jit(solution)/shard_map/rev | solution.py:101
  31.3 21.5 %fusion.49 = f32[1,256,2048]{2,0,1:T(1,128)S(1)} fusion(f32[1,383,2048]{2,1,0:T(8,128)S(1)} %convert_multiply_fusion, f32[128,1,2048]{2,0,1:T(8,128)S(1)} %bitcast.142), kind=kOutput, calls=%fused_computation.100 | convolution fusion | flops 805306368 | bytes 6283264 | tf_op jit(solution)/shard_map/conv_general_dilated | solution.py:19
  54.4 2.5 pad_maximum_fusion.6
  56.9 7.3 %copy.48 = f32[2,256,2048]{1,0,2:T(2,128)} copy(f32[2,256,2048]{2,1,0:T(8,128)} %pad_maximum_fusion.6) | data formatting | bytes 8388608 | tf_op jit(solution)/shard_map/stack | solution.py:108
  64.1 4.6 all-to-all-start
  68.8 49.0 %all-to-all-done = f32[2,256,2048]{1,0,2:T(2,128)} async-done(((f32[2,256,2048]{1,0,2:T(2,128)}), f32[2,256,2048]{1,0,2:T(2,128)}, u32[]{:S(2)}, u32[]{:S(2)}) %all-to-all-start) | async-done | bytes 4194336 | tf_op jit(solution)/shard_map/all_to_all | solution.py:107
  117.8 9.6 %fusion.58 = (f32[1,8,256,256]{2,0,3,1:T(1,128)}, f32[1,8,256,256]{2,0,3,1:T(1,128)}) fusion(f32[2,8,256,256]{2,0,3,1:T(2,128)} %bitcast.8), kind=kLoop, calls=%fused_computation.113 | loop fusion | bytes 8388608 | tf_op jit(solution)/shard_map/slice | solution.py:115
  127.4 4.5 copy.49
  131.9 6.0 %copy.50 = f32[1,8,256,256]{3,2,1,0:T(8,128)} copy(f32[1,8,256,256]{2,0,3,1:T(1,128)} %get-tuple-element.304) | data formatting | bytes 4194304 | tf_op jit(solution)/shard_map/slice | solution.py:115
  138.0 240.8 %while.19 = (s32[]{:T(128)}, f32[2048,256]{1,0:T(8,128)}, f32[2048,256]{1,0:T(8,128)}, f32[8,256]{1,0:T(8,128)S(1)}, f32[8,256]{1,0:T(8,128)S(1)}, /*index=5*/f3...) while((s32[]{:T(128)}, f32[2048,256]{1,0:T(8,128)}, ...), condition=%wide.region_2.3_spmd.clone.clone, body=%wide.region_0.2_spmd.clone.clone.sunk | while | flops 1617155328 | bytes 74435056 | solution.py:79
  143.8 3.5 fusion.80
  151.2 3.3 multiply_add_fusion.22
  155.4 4.0 fusion.89
  159.4 2.6 copy.106
  162.0 4.9 fusion.90
  172.8 3.5 fusion.80
  180.3 3.3 multiply_add_fusion.22
  184.4 4.0 fusion.89
  188.4 2.6 copy.106
  191.0 6.2 %fusion.90 = (f32[2048,256]{1,0:T(8,128)}, f32[2048,256]{1,0:T(8,128)}) fusion(f32[16,128,256]{2,1,0:T(8,128)} %copy.106, f32[2048,256]{1,0:T(8,128)} %get-tuple-element.414, f32[256]{0:T(256)S(1)} %bitcast.144, pred[]{:T(512)S(6)} %compare.24, f32[16,128,256]{2,1,0:T(8,128)} %multiply_add_fusion.22, f32[2048,256]{1,0:T(8,128)} %get-tuple-element.413), kind=kLoop, calls=%fused_computation.3.clone.1 | loop fusion | flops 3145728 | bytes 12583937 | tf_op jit(solution)/shard_map/while/body/eval_jaxpr/add | solution.py:69
  203.0 3.5 fusion.80
  210.5 3.3 multiply_add_fusion.22
  214.6 4.0 fusion.89
  218.7 2.6 copy.106
  221.3 6.2 %fusion.90 = (f32[2048,256]{1,0:T(8,128)}, f32[2048,256]{1,0:T(8,128)}) fusion(f32[16,128,256]{2,1,0:T(8,128)} %copy.106, f32[2048,256]{1,0:T(8,128)} %get-tuple-element.414, f32[256]{0:T(256)S(1)} %bitcast.144, pred[]{:T(512)S(6)} %compare.24, f32[16,128,256]{2,1,0:T(8,128)} %multiply_add_fusion.22, f32[2048,256]{1,0:T(8,128)} %get-tuple-element.413), kind=kLoop, calls=%fused_computation.3.clone.1 | loop fusion | flops 3145728 | bytes 12583937 | tf_op jit(solution)/shard_map/while/body/eval_jaxpr/add | solution.py:69
  233.3 3.5 fusion.80
  240.8 3.3 multiply_add_fusion.22
  244.9 4.0 fusion.89
  248.9 2.6 copy.106
  251.5 6.2 %fusion.90 = (f32[2048,256]{1,0:T(8,128)}, f32[2048,256]{1,0:T(8,128)}) fusion(f32[16,128,256]{2,1,0:T(8,128)} %copy.106, f32[2048,256]{1,0:T(8,128)} %get-tuple-element.414, f32[256]{0:T(256)S(1)} %bitcast.144, pred[]{:T(512)S(6)} %compare.24, f32[16,128,256]{2,1,0:T(8,128)} %multiply_add_fusion.22, f32[2048,256]{1,0:T(8,128)} %get-tuple-element.413), kind=kLoop, calls=%fused_computation.3.clone.1 | loop fusion | flops 3145728 | bytes 12583937 | tf_op jit(solution)/shard_map/while/body/eval_jaxpr/add | solution.py:69
  263.6 3.5 fusion.80
  271.0 3.3 multiply_add_fusion.22
  275.2 4.0 fusion.89
  279.2 2.6 copy.106
  281.8 6.2 %fusion.90 = (f32[2048,256]{1,0:T(8,128)}, f32[2048,256]{1,0:T(8,128)}) fusion(f32[16,128,256]{2,1,0:T(8,128)} %copy.106, f32[2048,256]{1,0:T(8,128)} %get-tuple-element.414, f32[256]{0:T(256)S(1)} %bitcast.144, pred[]{:T(512)S(6)} %compare.24, f32[16,128,256]{2,1,0:T(8,128)} %multiply_add_fusion.22, f32[2048,256]{1,0:T(8,128)} %get-tuple-element.413), kind=kLoop, calls=%fused_computation.3.clone.1 | loop fusion | flops 3145728 | bytes 12583937 | tf_op jit(solution)/shard_map/while/body/eval_jaxpr/add | solution.py:69
  293.8 3.5 fusion.80
  301.3 3.3 multiply_add_fusion.22
  305.4 4.0 fusion.89
  309.4 2.6 copy.106
  312.0 6.2 %fusion.90 = (f32[2048,256]{1,0:T(8,128)}, f32[2048,256]{1,0:T(8,128)}) fusion(f32[16,128,256]{2,1,0:T(8,128)} %copy.106, f32[2048,256]{1,0:T(8,128)} %get-tuple-element.414, f32[256]{0:T(256)S(1)} %bitcast.144, pred[]{:T(512)S(6)} %compare.24, f32[16,128,256]{2,1,0:T(8,128)} %multiply_add_fusion.22, f32[2048,256]{1,0:T(8,128)} %get-tuple-element.413), kind=kLoop, calls=%fused_computation.3.clone.1 | loop fusion | flops 3145728 | bytes 12583937 | tf_op jit(solution)/shard_map/while/body/eval_jaxpr/add | solution.py:69
  324.1 3.5 fusion.80
  331.5 3.3 multiply_add_fusion.22
  335.7 4.0 fusion.89
  339.7 2.6 copy.106
  342.3 6.2 %fusion.90 = (f32[2048,256]{1,0:T(8,128)}, f32[2048,256]{1,0:T(8,128)}) fusion(f32[16,128,256]{2,1,0:T(8,128)} %copy.106, f32[2048,256]{1,0:T(8,128)} %get-tuple-element.414, f32[256]{0:T(256)S(1)} %bitcast.144, pred[]{:T(512)S(6)} %compare.24, f32[16,128,256]{2,1,0:T(8,128)} %multiply_add_fusion.22, f32[2048,256]{1,0:T(8,128)} %get-tuple-element.413), kind=kLoop, calls=%fused_computation.3.clone.1 | loop fusion | flops 3145728 | bytes 12583937 | tf_op jit(solution)/shard_map/while/body/eval_jaxpr/add | solution.py:69
  354.3 3.5 fusion.80
  361.8 3.3 multiply_add_fusion.22
  365.9 4.0 fusion.89
  369.9 2.6 copy.106
  372.6 6.2 %fusion.90 = (f32[2048,256]{1,0:T(8,128)}, f32[2048,256]{1,0:T(8,128)}) fusion(f32[16,128,256]{2,1,0:T(8,128)} %copy.106, f32[2048,256]{1,0:T(8,128)} %get-tuple-element.414, f32[256]{0:T(256)S(1)} %bitcast.144, pred[]{:T(512)S(6)} %compare.24, f32[16,128,256]{2,1,0:T(8,128)} %multiply_add_fusion.22, f32[2048,256]{1,0:T(8,128)} %get-tuple-element.413), kind=kLoop, calls=%fused_computation.3.clone.1 | loop fusion | flops 3145728 | bytes 12583937 | tf_op jit(solution)/shard_map/while/body/eval_jaxpr/add | solution.py:69
  378.8 3.4 stack.21
  383.7 4.1 pad_maximum_fusion.7
  387.8 51.5 %all_to_all.30 = f32[2,2048,256]{2,0,1:T(2,128)S(1)} all-to-all(f32[2,2048,256]{2,0,1:T(2,128)S(1)} %pad_maximum_fusion.7), channel_id=1, replica_groups=mesh['ctx'=8,'tp'=4] {'ctx'}, dimensions={1} | all-to-all | bytes 8388608 | tf_op jit(solution)/shard_map/all_to_all | solution.py:117
  439.3 2.4 copy.97
  445.1 3.5 multiply_convert_fusion
  448.6 21.3 %fusion.46 = f32[1,128,2048]{2,0,1:T(1,128)S(1)} fusion(f32[256,1,2048]{2,0,1:T(8,128)S(1)} %bitcast.129, f32[1,383,2048]{2,1,0:T(8,128)S(1)} %copy-done.19), kind=kOutput, calls=%fused_computation.96 | convolution fusion | flops 805306368 | bytes 6283264 | tf_op jit(solution)/shard_map/conv_general_dilated | solution.py:19
  470.3 5.2 rev.16
  476.9 27.9 %all_gather.11 = f32[8,2048]{1,0:T(8,128)S(1)} all-gather(f32[8,256]{1,0:T(8,128)S(1)} %get-tuple-element.201), channel_id=1, replica_groups=mesh['ctx'=8,'tp'=4] {'ctx'}, dimensions={1}, use_global_device_ids=true | all-gather | bytes 73728 | tf_op jit(solution)/shard_map/all_gather | solution.py:122
  506.7 21.5 %fusion.38 = f32[1,256,2048]{2,0,1:T(1,128)S(1)} fusion(f32[1,383,2048]{2,1,0:T(8,128)S(1)} %maximum_bitcast_fusion, f32[128,1,2048]{2,0,1:T(8,128)S(1)} %bitcast.141), kind=kOutput, calls=%fused_computation.81 | convolution fusion | flops 805306368 | bytes 6283264 | tf_op jit(solution)/shard_map/conv_general_dilated | solution.py:19
  528.2 2.4 fusion.44
  530.6 5.2 all-gather.3.cloned.1.call-done
  535.7 4.2 reduce_sum.22
  (719 shorter events, 90.2 us)
Async XLA Ops:
  7.2 61.6 %copy-start = (f32[8,2048]{1,0:T(8,128)S(1)}, f32[8,2048]{1,0:T(8,128)}, u32[]{:S(2)}) copy-start(f32[8,2048]{1,0:T(8,128)} %param.19) | copy-start | bytes 196612
  7.2 20.7 %copy-start.9 = (bf16[256,2048]{1,0:T(8,128)(2,1)S(1)}, bf16[256,2048]{1,0:T(8,128)(2,1)}, u32[]{:S(2)}) copy-start(bf16[256,2048]{1,0:T(8,128)(2,1)} %param.12) | copy-start | bytes 3145732
  7.2 20.7 %copy-start.11 = (bf16[256,2048]{1,0:T(8,128)(2,1)S(1)}, bf16[256,2048]{1,0:T(8,128)(2,1)}, u32[]{:S(2)}) copy-start(bf16[256,2048]{1,0:T(8,128)(2,1)} %param.13) | copy-start | bytes 3145732
  9.3 18.5 %collective-permute-start = (bf16[127,2048]{1,0:T(8,128)(2,1)}, bf16[127,2048]{1,0:T(8,128)(2,1)S(1)}, u32[]{:S(2)}, u32[]{:S(2)}) collective-permute-start(bf16[127,2048]{1,0:T(8,128)(2,1)} %slice.393), channel_id=1, source_target_pairs={{0,4},{4,8},{8,12},{12,16},{16,20},{20,24},{24,28},{1,5},{5,9},{9,... | collective-permute-start | bytes 1560584 | tf_op jit(solution)/shard_map/ppermute | solution.py:14
  13.7 14.1 %collective-permute-start.1 = (bf16[127,2048]{1,0:T(8,128)(2,1)}, bf16[127,2048]{1,0:T(8,128)(2,1)}, u32[]{:S(2)}, u32[]{:S(2)}) collective-permute-start(bf16[127,2048]{1,0:T(8,128)(2,1)} %slice.394), channel_id=1, source_target_pairs={{0,4},{4,8},{8,12},{12,16},{16,20},{20,24},{24,28},{1,5},{5,9},{9,... | collective-permute-start | bytes 1560584 | tf_op jit(solution)/shard_map/ppermute | solution.py:14
  27.9 3.4 copy-start.22
  29.6 1.6 copy-start.18
  31.3 21.6 %copy-start.13 = (bf16[256,2048]{1,0:T(8,128)(2,1)S(1)}, bf16[256,2048]{1,0:T(8,128)(2,1)}, u32[]{:S(2)}) copy-start(bf16[256,2048]{1,0:T(8,128)(2,1)} %param.15) | copy-start | bytes 3145732
  31.3 21.6 %copy-start.14 = (bf16[256,2048]{1,0:T(8,128)(2,1)S(1)}, bf16[256,2048]{1,0:T(8,128)(2,1)}, u32[]{:S(2)}) copy-start(bf16[256,2048]{1,0:T(8,128)(2,1)} %param.11) | copy-start | bytes 3145732
  31.3 21.6 %copy-start.16 = (bf16[256,2048]{1,0:T(8,128)(2,1)S(1)}, bf16[256,2048]{1,0:T(8,128)(2,1)}, u32[]{:S(2)}) copy-start(bf16[256,2048]{1,0:T(8,128)(2,1)} %param.16) | copy-start | bytes 3145732
  31.3 21.6 %copy-start.20 = (bf16[256,2048]{1,0:T(8,128)(2,1)S(1)}, bf16[256,2048]{1,0:T(8,128)(2,1)}, u32[]{:S(2)}) copy-start(bf16[256,2048]{1,0:T(8,128)(2,1)} %param.14) | copy-start | bytes 3145732
  52.9 1.5 copy-start.7
  64.1 53.7 %all-to-all-start = ((f32[2,256,2048]{1,0,2:T(2,128)}), f32[2,256,2048]{1,0,2:T(2,128)}, u32[]{:S(2)}, u32[]{:S(2)}) async-start(f32[2,256,2048]{1,0,2:T(2,128)} %copy.48), calls=%async_computation | async-start | bytes 8388608 | tf_op jit(solution)/shard_map/all_to_all | solution.py:107
  68.7 467.1 %all-gather.3.cloned.1.call-start = ((), (), s32[]{:S(2)}) async-start(), calls=%async_computation.2 | async-start | bytes 9437184 | tf_op jit(solution)/shard_map/all_gather | solution.py:133
  131.9 6.1 %copy-start.23 = (f32[8]{0:T(128)S(1)}, f32[8]{0:T(128)}, u32[]{:S(2)}) copy-start(f32[8]{0:T(128)} %param.18) | copy-start | bytes 100
  138.0 4.1 copy-start.2
  142.1 1.3 copy-start.4
  148.5 1.4 copy-start.6
  162.0 5.0 copy-start.3
  167.0 4.1 copy-start.2
  171.1 1.3 copy-start.4
  177.5 1.4 copy-start.6
  191.0 6.2 %copy-start.3 = (f32[2048,256]{1,0:T(8,128)S(1)}, f32[2048,256]{1,0:T(8,128)}, u32[]{:S(2)}) copy-start(f32[2048,256]{1,0:T(8,128)} %copy-done.2) | copy-start | bytes 6291460 | tf_op jit(solution)/shard_map/while
  197.2 4.1 copy-start.2
  201.3 1.3 copy-start.4
  207.8 1.4 copy-start.6
  221.3 6.2 %copy-start.3 = (f32[2048,256]{1,0:T(8,128)S(1)}, f32[2048,256]{1,0:T(8,128)}, u32[]{:S(2)}) copy-start(f32[2048,256]{1,0:T(8,128)} %copy-done.2) | copy-start | bytes 6291460 | tf_op jit(solution)/shard_map/while
  227.5 4.1 copy-start.2
  231.6 1.3 copy-start.4
  238.0 1.4 copy-start.6
  251.5 6.2 %copy-start.3 = (f32[2048,256]{1,0:T(8,128)S(1)}, f32[2048,256]{1,0:T(8,128)}, u32[]{:S(2)}) copy-start(f32[2048,256]{1,0:T(8,128)} %copy-done.2) | copy-start | bytes 6291460 | tf_op jit(solution)/shard_map/while
  257.8 4.1 copy-start.2
  261.8 1.3 copy-start.4
  268.3 1.4 copy-start.6
  281.8 6.2 %copy-start.3 = (f32[2048,256]{1,0:T(8,128)S(1)}, f32[2048,256]{1,0:T(8,128)}, u32[]{:S(2)}) copy-start(f32[2048,256]{1,0:T(8,128)} %copy-done.2) | copy-start | bytes 6291460 | tf_op jit(solution)/shard_map/while
  288.0 4.1 copy-start.2
  292.1 1.3 copy-start.4
  298.5 1.4 copy-start.6
  312.0 6.2 %copy-start.3 = (f32[2048,256]{1,0:T(8,128)S(1)}, f32[2048,256]{1,0:T(8,128)}, u32[]{:S(2)}) copy-start(f32[2048,256]{1,0:T(8,128)} %copy-done.2) | copy-start | bytes 6291460 | tf_op jit(solution)/shard_map/while
  318.3 4.1 copy-start.2
  322.4 1.3 copy-start.4
  328.8 1.4 copy-start.6
  342.3 6.2 %copy-start.3 = (f32[2048,256]{1,0:T(8,128)S(1)}, f32[2048,256]{1,0:T(8,128)}, u32[]{:S(2)}) copy-start(f32[2048,256]{1,0:T(8,128)} %copy-done.2) | copy-start | bytes 6291460 | tf_op jit(solution)/shard_map/while
  348.5 4.1 copy-start.2
  352.6 1.3 copy-start.4
  359.0 1.4 copy-start.6
  372.6 6.2 %copy-start.3 = (f32[2048,256]{1,0:T(8,128)S(1)}, f32[2048,256]{1,0:T(8,128)}, u32[]{:S(2)}) copy-start(f32[2048,256]{1,0:T(8,128)} %copy-done.2) | copy-start | bytes 6291460 | tf_op jit(solution)/shard_map/while
  378.8 3.4 copy-start.5
  442.9 1.6 copy-start.8
  442.9 1.8 copy-start.15
  443.0 2.1 copy-start.17
  445.1 3.5 copy-start.19
  475.6 29.9 %collective-permute-start.2 = (f32[127,2048]{1,0:T(8,128)S(1)}, f32[127,2048]{1,0:T(8,128)S(1)}, u32[]{:S(2)}, u32[]{:S(2)}) collective-permute-start(f32[127,2048]{1,0:T(8,128)S(1)} %slice.517), channel_id=1, source_target_pairs={{4,0},{8,4},{12,8},{16,12},{20,16},{24,20},{28,24},{5,1},{9,5},{13... | collective-permute-start | bytes 3121160 | tf_op jit(solution)/shard_map/ppermute | solution.py:14
  505.4 1.2 copy-start.21
  506.7 21.5 %copy-start.10 = (bf16[256,2048]{1,0:T(8,128)(2,1)S(1)}, bf16[256,2048]{1,0:T(8,128)(2,1)}, u32[]{:S(2)}) copy-start(bf16[256,2048]{1,0:T(8,128)(2,1)} %param.12) | copy-start | bytes 3145732
  506.7 21.5 %copy-start.12 = (bf16[256,2048]{1,0:T(8,128)(2,1)S(1)}, bf16[256,2048]{1,0:T(8,128)(2,1)}, u32[]{:S(2)}) copy-start(bf16[256,2048]{1,0:T(8,128)(2,1)} %param.13) | copy-start | bytes 3145732
  535.7 5.3 copy-start.1
Sparse Core Ops, SparseCore 0:
  475.6 60.0 all-gather.2
